TPU v7x, 32 devices: a whole 2x2x4 slice. The times are simulated.
32 devices in a mesh: gy: 8 (over z, core), gz: 4 (over y, x).
Axes of the slice: x: 2, y: 2, z: 4, core: 2. Of those that a mesh axis runs over, the one named last changes fastest.
Arguments:
- state_field: bfloat16 [11, 64, 256, 512], P(None, 'gz', 'gy'), may hold values from -100 to 100, as said below
- start_factor: float32 [512, 64], replicated, may hold values from -6 to 6
Outputs:
- factor_one: float32 [512, 64], replicated
- mode_two_gram: float32 [256, 256], P('gy')
Inputs may be any that keep to these rules, and one draw needn't show every extreme that they name: `state_field`: Real-valued field of full rank along every mode.
All inputs are finite; a program needn't handle non-finite values.
Results may differ from a plain program's by a relative error of at most 0.00052.
Values may be sent and summed in bfloat16 or wider, within the bound.
A program may use at most 64 MiB of HBM per device.

v0:
```python
import functools

import jax
import jax.numpy as jnp
from jax import lax
from jax.experimental import pallas as pl
from jax.experimental.pallas import tpu as pltpu
from jax.sharding import PartitionSpec as P

ITERS = 6
AHEAD = 1
MESH = pl.DeviceIdType.MESH
LANES = 128
VMEM = pl.BlockSpec(memory_space=pltpu.VMEM)
NT = (((1,), (1,)), ((), ()))


def greet(partners):
    barrier = pltpu.get_barrier_semaphore()
    for partner in partners:
        pl.semaphore_signal(barrier, inc=1, device_id=partner, device_id_type=MESH)
    pl.semaphore_wait(barrier, len(partners))


def send(src, dst, send_sem, recv_sem, device):
    copy = pltpu.make_async_remote_copy(
        src_ref=src, dst_ref=dst, send_sem=send_sem, recv_sem=recv_sem,
        device_id=device, device_id_type=MESH,
    )
    copy.start()
    return copy


def sum_kernel(ny, nz, chunk, g_ref, out_ref, packed, got1, held, got2, mid, got3, full,
               s1, r1, s2, r2, s3, r3, s4, r4, s5, r5, s6, r6):
    gy, gz = lax.axis_index("gy"), lax.axis_index("gz")
    depth = ny // 2
    zi, core = gy // 2, gy % 2
    rows2 = depth * chunk
    partner = (gy + 1 - 2 * core, gz)
    planes = [lax.rem(gz + o, nz) for o in range(nz)]
    stacks = [lax.rem(zi + o, depth) for o in range(depth)]

    def part(half, g):
        return pl.ds(pl.multiple_of((half * nz + g) * rows2, 8), rows2)

    n = g_ref.shape[0] // LANES
    blocks = [(i, j) for i in range(n) for j in range(i, n)]
    for k, (i, j) in enumerate(blocks):
        packed[k * LANES:(k + 1) * LANES, :] = g_ref[i * LANES:(i + 1) * LANES, j * LANES:(j + 1) * LANES]
    used = len(blocks) * LANES
    if used < packed.shape[0]:
        packed[used:, :] = jnp.zeros((packed.shape[0] - used, LANES), jnp.float32)

    greet([partner] + [(gy, g) for g in planes[1:]] + [(2 * q + core, gz) for q in stacks[1:]])

    order = list(range(1, nz)) + [0]
    copies = []
    first = {}
    for o in order:
        first[o] = send(packed.at[part(1 - core, planes[o])], got1.at[o], s1.at[o], r1.at[o], partner)
    second = {}
    for o in order:
        first[o].wait_recv()
        held[o] = packed[part(core, planes[o]), :] + got1[o]
        if o:
            second[o] = send(held.at[o], got2.at[o], s2.at[o], r2.at[o], (gy, planes[o]))
    total = held[0]
    for o in range(1, nz):
        second[o].wait_recv()
        total = total + got2[o]
    mid[...] = total
    third = {}
    for o in range(1, depth):
        rows = pl.ds(pl.multiple_of(stacks[o] * chunk, 8), chunk)
        third[o] = send(mid.at[rows], got3.at[o], s3.at[o], r3.at[o], (2 * stacks[o] + core, gz))
    piece = mid[pl.ds(pl.multiple_of(zi * chunk, 8), chunk), :]
    for o in range(1, depth):
        third[o].wait_recv()
        piece = piece + got3[o]
    mine = pl.ds(pl.multiple_of((core * nz + gz) * rows2 + zi * chunk, 8), chunk)
    full[mine, :] = piece
    fourth = {}
    for o in range(1, depth):
        fourth[o] = send(full.at[mine], full.at[mine], s4.at[o], r4.at[o], (2 * stacks[o] + core, gz))
    for o in range(1, depth):
        fourth[o].wait_recv()
    own = part(core, gz)
    fifth, sixth = {}, {}
    for o in range(1, nz):
        fifth[o] = send(full.at[own], full.at[own], s5.at[o], r5.at[o], (gy, planes[o]))
    sixth[0] = send(full.at[own], full.at[own], s6.at[0], r6.at[0], partner)
    for o in range(1, nz):
        fifth[o].wait_recv()
        came = part(core, lax.rem(gz + nz - o, nz))
        sixth[o] = send(full.at[came], full.at[came], s6.at[o], r6.at[o], partner)
    for o in range(nz):
        sixth[o].wait_recv()
    for group in (first, second, third, fourth, fifth, sixth):
        for copy in group.values():
            copy.wait_send()
    for k, (i, j) in enumerate(blocks):
        block = full[k * LANES:(k + 1) * LANES, :]
        out_ref[i * LANES:(i + 1) * LANES, j * LANES:(j + 1) * LANES] = block
        if i != j:
            out_ref[j * LANES:(j + 1) * LANES, i * LANES:(i + 1) * LANES] = block.T


def sum_over_devices(partial_gram):
    ny, nz = lax.axis_size("gy"), lax.axis_size("gz")
    n = partial_gram.shape[0] // LANES
    used = n * (n + 1) // 2 * LANES
    devices = ny * nz
    chunk = -(-used // (8 * devices)) * 8
    depth = ny // 2
    rows2 = depth * chunk
    f32 = jnp.float32
    dma = pltpu.SemaphoreType.DMA
    return pl.pallas_call(
        functools.partial(sum_kernel, ny, nz, chunk),
        out_shape=jax.ShapeDtypeStruct(partial_gram.shape, f32),
        in_specs=[VMEM], out_specs=VMEM,
        scratch_shapes=[
            pltpu.VMEM((chunk * devices, LANES), f32),
            pltpu.VMEM((nz, rows2, LANES), f32),
            pltpu.VMEM((nz, rows2, LANES), f32),
            pltpu.VMEM((nz, rows2, LANES), f32),
            pltpu.VMEM((rows2, LANES), f32),
            pltpu.VMEM((depth, chunk, LANES), f32),
            pltpu.VMEM((chunk * devices, LANES), f32),
        ] + [dma((nz,))] * 4 + [dma((depth,))] * 4 + [dma((nz,))] * 4,
        compiler_params=pltpu.CompilerParams(collective_id=0, has_side_effects=True),
        name="sum_gram",
    )(partial_gram)


def split(value):
    high = value.astype(jnp.bfloat16)
    rest = value - high.astype(jnp.float32)
    mid = rest.astype(jnp.bfloat16)
    low = (rest - mid.astype(jnp.float32)).astype(jnp.bfloat16)
    return high, mid, low


def dot(a, b, dims=(((1,), (0,)), ((), ()))):
    return lax.dot_general(a, b, dims, preferred_element_type=jnp.float32)


def inverse_lower(c):
    r1 = c.shape[0]
    nb = r1 // 8
    wide = 2 * r1
    row = lax.broadcasted_iota(jnp.int32, (r1, r1), 0)
    col = lax.broadcasted_iota(jnp.int32, (r1, r1), 1)
    whole = jnp.concatenate([c, (row == col).astype(jnp.float32)], axis=1)
    m = [whole[8 * i:8 * i + 8, :] for i in range(nb)]
    sub = lax.broadcasted_iota(jnp.int32, (8, wide), 0)
    result = []
    for b in range(nb):
        cols = [
            [jnp.broadcast_to(m[i][:, 8 * b + k:8 * b + k + 1], (8, wide)) for i in range(b, nb)]
            for k in range(8)
        ]
        done = jnp.zeros((8, wide), jnp.float32)
        for k in range(8):
            d = jnp.broadcast_to(cols[k][0][k:k + 1, :], (8, wide))
            r = lax.rsqrt(d)
            inv = r * r
            ratio = [v * inv for v in cols[k]]
            u = jnp.broadcast_to(m[b][k:k + 1, :], (8, wide))
            done = jnp.where(sub == k, u * r, done)
            for k2 in range(k + 1, 8):
                s = jnp.broadcast_to(cols[k][0][k2:k2 + 1, :], (8, wide))
                cols[k2] = [v - l * s for v, l in zip(cols[k2], ratio)]
            for i in range(b, nb):
                m[i] = m[i] - ratio[i - b] * u
        result.append(done[:, r1:])
    return jnp.concatenate(result, axis=0)


def iteration(g1, g2, g3, held, _, carry):
    r1 = held.shape[0]
    f1, f2, f3 = split(held[...])
    t1 = dot(jnp.concatenate([f1, f2, f3], axis=0), g1[...])
    t2 = dot(jnp.concatenate([f1, f2], axis=0), g2[...])
    t3 = dot(f1, g3[...])
    a = t1[:r1] + ((t1[r1:2 * r1] + t2[:r1]) + (t1[2 * r1:] + t2[r1:] + t3))
    a1, a2, a3 = split(a)
    stack = jnp.concatenate([a1, a2, a3], axis=0)
    c = dot(a1, a1, NT) + (
        dot(a1, a2, NT) + dot(a2, a1, NT) + (dot(a2, a2, NT) + dot(a1, a3, NT) + dot(a3, a1, NT))
    )
    w1, w2, w3 = split(inverse_lower(c))
    none = jnp.zeros_like(w1)
    t = dot(
        jnp.concatenate(
            [
                jnp.concatenate([w1, w1, w1], axis=1),
                jnp.concatenate([w2, w2, none], axis=1),
                jnp.concatenate([w3, none, none], axis=1),
            ],
            axis=0,
        ),
        stack,
    )
    held[...] = t[:r1] + (t[r1:2 * r1] + t[2 * r1:])
    return carry


def iterate_kernel(g_ref, f_ref, out_ref, g1, g2, g3, held):
    g1[...], g2[...], g3[...] = split(g_ref[...])
    held[...] = f_ref[...].T
    lax.fori_loop(0, ITERS, functools.partial(iteration, g1, g2, g3, held), 0)
    out_ref[...] = held[...].T


def iterate(mode_gram, start_factor):
    n, r1 = start_factor.shape
    return pl.pallas_call(
        iterate_kernel,
        out_shape=jax.ShapeDtypeStruct((n, r1), jnp.float32),
        in_specs=[VMEM, VMEM], out_specs=VMEM,
        scratch_shapes=[pltpu.VMEM((n, n), jnp.bfloat16)] * 3 + [pltpu.VMEM((r1, n), jnp.float32)],
        name="subspace",
    )(mode_gram, start_factor)


def whole_kernel(ny, nz, chunk, jb, ahead, scale, x_ref, f_ref, factor_ref, out_ref,
                 xs, acc, packed, got1, held, got2, mid, got3, full, g1, g2, g3, basis, weights,
                 raw, mine, z, gram, got4, part, got5, last,
                 xsem, s1, r1, s2, r2, s3, r3, s4, r4, s5, r5, s6, r6, sr, rr,
                 sa, ra, sb, rb, sc, rc, sd, rd):
    gy, gz = lax.axis_index("gy"), lax.axis_index("gz")
    depth = ny // 2
    zi, core = gy // 2, gy % 2
    partner = (gy + 1 - 2 * core, gz)
    planes = [lax.rem(gz + o, nz) for o in range(nz)]
    stacks = [lax.rem(zi + p, depth) for p in range(depth)]
    peers = [lax.rem(gy + o, ny) for o in range(ny)]
    rows = mine.shape[1]
    early = ahead * jb
    n1 = x_ref.shape[2]
    copies = []

    barrier = pltpu.get_barrier_semaphore()
    greeted = [(p, gz) for p in peers[1:]] + [(gy, g) for g in planes[1:]]
    for device in greeted:
        pl.semaphore_signal(barrier, inc=1, device_id=device, device_id_type=MESH)

    def load(o):
        src = x_ref.at[:, pl.ds(pl.multiple_of(peers[o] * rows, 8), rows)]
        return pltpu.make_async_copy(src, xs.at[o], xsem.at[o])

    loads = [load(o) for o in range(ny)]
    for copy in loads:
        copy.start()

    size = 2 * LANES
    for o in range(ny):
        loads[o].wait()
        for i in range(0, n1, size):
            left = xs[o, :, :, i:i + size].reshape(2 * rows, size)
            right = xs[o, :, :, i:].reshape(2 * rows, n1 - i)
            value = dot(left, right, (((0,), (0,)), ((), ())))
            if o:
                acc[i:i + size, i:] += value
            else:
                acc[i:i + size, i:] = value

    n = n1 // LANES
    blocks = [(i, j) for i in range(n) for j in range(i, n)]
    for k, (i, j) in enumerate(blocks):
        packed[k * LANES:(k + 1) * LANES, :] = acc[i * LANES:(i + 1) * LANES, j * LANES:(j + 1) * LANES]
    used = len(blocks) * LANES
    if used < packed.shape[0]:
        packed[used:, :] = jnp.zeros((packed.shape[0] - used, LANES), jnp.float32)

    pl.semaphore_wait(barrier, len(greeted))

    unit = nz * chunk

    def span(half, q):
        return pl.ds(pl.multiple_of((half * depth + q) * unit, 8), unit)

    def spot(half, q, g):
        return pl.ds(pl.multiple_of((half * depth + q) * unit + g * chunk, 8), chunk)

    order = list(range(depth - 1, 0, -1)) + [0]
    first, second, third = {}, {}, {}
    for p in order:
        first[p] = send(packed.at[span(1 - core, stacks[p])], got1.at[p], s1.at[p], r1.at[p], partner)
    for p in order:
        first[p].wait_recv()
        held[p] = packed[span(core, stacks[p]), :] + got1[p]
        for o in range(1, nz):
            rows_o = pl.ds(pl.multiple_of(planes[o] * chunk, 8), chunk)
            second[p, o] = send(held.at[p, rows_o], got2.at[p, o], s2.at[p, o], r2.at[p, o], (gy, planes[o]))
    piece = None
    for p in order:
        total = held[p, pl.ds(pl.multiple_of(gz * chunk, 8), chunk), :]
        for o in range(1, nz):
            second[p, o].wait_recv()
            total = total + got2[p, o]
        if p:
            mid[p] = total
            third[p] = send(mid.at[p], got3.at[p], s3.at[p], r3.at[p], (2 * stacks[p] + core, gz))
        else:
            piece = total
    for p in range(1, depth):
        third[p].wait_recv()
        piece = piece + got3[p]
    own = spot(core, zi, gz)
    full[own, :] = piece
    fourth, fifth, sixth = {}, {}, {}
    for p in range(1, depth):
        fourth[p] = send(full.at[own], full.at[own], s4.at[p], r4.at[p], (2 * stacks[p] + core, gz))
    came = [lax.rem(zi + depth - p, depth) for p in range(depth)]
    for p in range(depth):
        if p:
            fourth[p].wait_recv()
        here = spot(core, came[p], gz)
        for o in range(1, nz):
            fifth[p, o] = send(full.at[here], full.at[here], s5.at[p, o], r5.at[p, o], (gy, planes[o]))
    for p in range(depth):
        for o in range(1, nz):
            fifth[p, o].wait_recv()
        here = span(core, came[p])
        sixth[p] = send(full.at[here], full.at[here], s6.at[p], r6.at[p], partner)
    for p in range(depth):
        sixth[p].wait_recv()

    sent = {}
    if ahead:
        for o in range(1, ny):
            sent[o] = send(xs.at[o, :, pl.ds(0, early)], raw.at[gy], sr.at[o], rr.at[o], (peers[o], gz))

    for k, (i, j) in enumerate(blocks):
        block = full[k * LANES:(k + 1) * LANES, :]
        for a, b, value in ((i, j, block), (j, i, block.T))[:1 if i == j else 2]:
            where = (slice(a * LANES, (a + 1) * LANES), slice(b * LANES, (b + 1) * LANES))
            g1[where], g2[where], g3[where] = split(value)
    basis[...] = f_ref[...]
    lax.fori_loop(0, ITERS, functools.partial(iteration, g1, g2, g3, basis), 0)
    factor = basis[...]
    factor_ref[...] = factor
    narrow = factor.T.astype(jnp.bfloat16)
    empty = jnp.zeros_like(narrow)
    weights[0] = jnp.concatenate([narrow, empty], axis=1)
    weights[1] = jnp.concatenate([empty, narrow], axis=1)

    def project(pair):
        return (dot(pair[0], weights[0]) + dot(pair[1], weights[1])).astype(jnp.bfloat16)

    across = {}
    far = list(range(ny // 2, ny)) + list(range(ny // 2 - 1, 0, -1))
    for o in far:
        mine[o, early:] = project(xs[o, :, early:])
        across[o] = send(
            mine.at[o, pl.ds(early, rows - early)], z.at[gy, pl.ds(early, rows - early)],
            sa.at[o], ra.at[o], (peers[o], gz),
        )
    z[gy] = project(xs[0])
    if ahead:
        for o in range(1, ny):
            sent[o].wait_recv()
            source = lax.rem(gy + ny - o, ny)
            z[source, :early] = project(raw[source])
    for o in range(1, ny):
        across[o].wait_recv()
    wide = jnp.concatenate(
        [z[:, t * jb:(t + 1) * jb, :].reshape(ny * jb, LANES) for t in range(rows // jb)], axis=1
    )
    gram[...] = dot(wide, wide, NT).reshape(gram.shape)
    planar, rowwise, final = {}, {}, {}
    far = far + [0]
    for o in far:
        for g in range(1, nz):
            planar[o, g] = send(
                gram.at[peers[o], planes[g]], got4.at[o, g], sb.at[o, g], rb.at[o, g], (gy, planes[g])
            )
    for o in far:
        total = gram[peers[o], gz]
        for g in range(1, nz):
            planar[o, g].wait_recv()
            total = total + got4[o, g]
        if o:
            part[o] = total
            rowwise[o] = send(part.at[o], got5.at[o], sc.at[o], rc.at[o], (peers[o], gz))
    for o in range(1, ny):
        rowwise[o].wait_recv()
        total = total + got5[o]
    last[gz] = total * scale
    for o in range(1, nz):
        final[o] = send(last.at[gz], last.at[gz], sd.at[o], rd.at[o], (gy, planes[o]))
    for o in range(1, nz):
        final[o].wait_recv()
    for group in (first, second, third, fourth, fifth, sixth, sent, across, planar, rowwise, final):
        for copy in group.values():
            copy.wait_send()
    out_ref[...] = last[...]


def whole(state_field, start_factor, divisor):
    ny, nz = lax.axis_size("gy"), lax.axis_size("gz")
    nv, nk, jb, n1 = state_field.shape
    r1 = start_factor.shape[1]
    half = nv * nk // 2
    rows = half // ny * jb
    ahead = AHEAD
    halves = state_field.reshape(2, half * jb, n1)
    n = n1 // LANES
    used = n * (n + 1) // 2 * LANES
    chunk = -(-used // (8 * ny * nz)) * 8
    depth = ny // 2
    unit = nz * chunk
    q, j2 = jb // nz, ny * jb
    f32, bf16 = jnp.float32, jnp.bfloat16
    dma = pltpu.SemaphoreType.DMA
    vmem = pltpu.VMEM
    factor, out = pl.pallas_call(
        functools.partial(whole_kernel, ny, nz, chunk, jb, ahead, 1.0 / divisor),
        out_shape=(jax.ShapeDtypeStruct((r1, n1), f32), jax.ShapeDtypeStruct((nz, q, j2), f32)),
        in_specs=[pl.BlockSpec(memory_space=pl.ANY), VMEM], out_specs=(VMEM, VMEM),
        scratch_shapes=[
            vmem((ny, 2, rows, n1), bf16),
            vmem((n1, n1), f32),
            vmem((chunk * ny * nz, LANES), f32),
            vmem((depth, unit, LANES), f32),
            vmem((depth, unit, LANES), f32),
            vmem((depth, nz, chunk, LANES), f32),
            vmem((depth, chunk, LANES), f32),
            vmem((depth, chunk, LANES), f32),
            vmem((chunk * ny * nz, LANES), f32),
            vmem((n1, n1), bf16), vmem((n1, n1), bf16), vmem((n1, n1), bf16),
            vmem((r1, n1), f32),
            vmem((2, n1, LANES), bf16),
            vmem((ny, 2, max(ahead, 1) * jb, n1), bf16),
            vmem((ny, rows, LANES), bf16),
            vmem((ny, rows, LANES), bf16),
            vmem((ny, nz, q, j2), f32),
            vmem((ny, nz, q, j2), f32),
            vmem((ny, q, j2), f32),
            vmem((ny, q, j2), f32),
            vmem((nz, q, j2), f32),
            dma((ny,)),
        ] + [dma((depth,))] * 2 + [dma((depth, nz))] * 2 + [dma((depth,))] * 4 + [dma((depth, nz))] * 2
        + [dma((depth,))] * 2 + [dma((ny,))] * 4 + [dma((ny, nz))] * 2 + [dma((ny,))] * 2 + [dma((nz,))] * 2,
        compiler_params=pltpu.CompilerParams(
            collective_id=1, has_side_effects=True, vmem_limit_bytes=56 * 2**20
        ),
        name="whole",
    )(halves, start_factor.T)
    return factor.T, out.reshape(jb, j2)


def second_gram_plain(state_field, narrow, divisor):
    shrunk = jnp.einsum(
        "vkji,ir->jvkr", state_field, narrow, preferred_element_type=jnp.float32
    ).astype(jnp.bfloat16)
    matrix = shrunk.reshape(shrunk.shape[0], -1)
    columns = lax.all_to_all(matrix, "gy", split_axis=1, concat_axis=0, tiled=True)
    partial_two = lax.psum_scatter(dot(columns, columns, NT), "gy", scatter_dimension=0, tiled=True)
    return lax.psum(partial_two, "gz") / divisor


def per_device(state_field, start_factor):
    ny, nz = lax.axis_size("gy"), lax.axis_size("gz")
    nv, nk, jb, n1 = state_field.shape
    r1 = start_factor.shape[1]
    divisor = nv * nk * nz * r1
    if (nv * nk) % (2 * ny) == 0 and jb % (8 * nz) == 0 and 2 * r1 == LANES and n1 % (2 * LANES) == 0:
        return whole(state_field, start_factor, divisor)
    flattened = state_field.reshape(-1, n1)
    partial_value = dot(flattened, flattened, (((0,), (0,)), ((), ())))
    factor_one = iterate(sum_over_devices(partial_value), start_factor)
    return (factor_one, second_gram_plain(state_field, factor_one.astype(jnp.bfloat16), divisor))


def solution(mesh):
    placed = (P(None, "gz", "gy", None), P())
    return jax.shard_map(
        per_device, mesh=mesh, in_specs=placed, out_specs=(P(), P("gy", None)), check_vma=False
    )
```

profile of v0, /device:TPU:0, one launch (start us, length us, event | category | flops | bytes accessed | tf_op | source)
XLA Modules:
  0.0 77.4 jit_solution(287390802513154568)
XLA Ops:
  0.6 73.8 %whole.1 = (f32[64,512]{1,0:T(8,128)}, f32[4,8,256]{2,1,0:T(8,128)}) custom-call(bf16[2,2816,512]{2,1,0:T(8,128)(2,1)} %bitcast.4, f32[64,512]{1,0:T(8,128)} %bitcast.5), custom_call_target="tpu_custom_call" | custom-call | tf_op jit(solution)/shard_map/whole/pallas_call | solution.py:420
  74.4 1.6 %copy.6 = f32[512,64]{0,1:T(8,128)} copy(f32[512,64]{0,1:T(8,128)} %bitcast.6) | data formatting | bytes 262144
  76.0 1.4 %copy.7 = f32[32,256]{1,0:T(8,128)} copy(f32[32,256]{1,0:T(8,128)} %bitcast.7) | data formatting | bytes 65536
where the time goes:
time: 77.6 us; the launch traced here: 77.4 us
  Pallas kernels  73.8 us (95%)
  local copies, waits for them, and re-layouts  2.94 us (4%)
    pallas_call x1, Pallas kernels, whole(): pl.pallas_call(functools.partial(whole_kernel, ny, nz, chunk, jb, ahead,...  73.8 us
    unnamed x2, local copies, waits for them, and re-layouts  2.94 us

commit v1 on v0

--- a/solution.py
+++ b/solution.py
@@ -12,6 +12,7 @@
 MESH = pl.DeviceIdType.MESH
 LANES = 128
 VMEM = pl.BlockSpec(memory_space=pltpu.VMEM)
+ANY = pl.BlockSpec(memory_space=pl.ANY)
 NT = (((1,), (1,)), ((), ()))
 
 
@@ -146,6 +147,14 @@
     return lax.dot_general(a, b, dims, preferred_element_type=jnp.float32)
 
 
+def rows_of(tile, k):
+    return jnp.broadcast_to(tile[k:k + 1, :], tile.shape)
+
+
+def lanes_of(tile, k):
+    return jnp.take_along_axis(tile, jnp.full(tile.shape, k, jnp.int32), axis=1, mode="promise_in_bounds")
+
+
 def inverse_lower(c):
     r1 = c.shape[0]
     nb = r1 // 8
@@ -155,41 +164,69 @@
     whole = jnp.concatenate([c, (row == col).astype(jnp.float32)], axis=1)
     m = [whole[8 * i:8 * i + 8, :] for i in range(nb)]
     sub = lax.broadcasted_iota(jnp.int32, (8, wide), 0)
+    lane = lax.broadcasted_iota(jnp.int32, (8, wide), 1)
+    diag = [lanes_of(m[0], k) for k in range(8)]
+    root = lax.rsqrt(rows_of(diag[0], 0))
+    unit = root * root
+    scale = jnp.where(lane < r1, unit, root)
+    diag = [v * unit for v in diag]
     result = []
     for b in range(nb):
-        cols = [
-            [jnp.broadcast_to(m[i][:, 8 * b + k:8 * b + k + 1], (8, wide)) for i in range(b, nb)]
-            for k in range(8)
-        ]
-        done = jnp.zeros((8, wide), jnp.float32)
-        for k in range(8):
-            d = jnp.broadcast_to(cols[k][0][k:k + 1, :], (8, wide))
-            r = lax.rsqrt(d)
+        cols = [[diag[k]] + [lanes_of(m[i], 8 * b + k) for i in range(b + 1, nb)] for k in range(8)]
+        after = [lanes_of(m[b + 1], 8 * (b + 1) + k) for k in range(8)] if b + 1 < nb else []
+        if b == 0:
+            cols = [v[:1] + [x * unit for x in v[1:]] for v in cols]
+            after = [x * unit for x in after]
+            m = [x * scale for x in m]
+        done = None
+        for k in range(0, 8, 2):
+            x, y = cols[k], cols[k + 1]
+            p, q = x[0], y[0]
+            a, e, d = rows_of(p, k), rows_of(p, k + 1), rows_of(q, k + 1)
+            r = lax.rsqrt(a * d - e * e)
             inv = r * r
-            ratio = [v * inv for v in cols[k]]
-            u = jnp.broadcast_to(m[b][k:k + 1, :], (8, wide))
-            done = jnp.where(sub == k, u * r, done)
-            for k2 in range(k + 1, 8):
-                s = jnp.broadcast_to(cols[k][0][k2:k2 + 1, :], (8, wide))
-                cols[k2] = [v - l * s for v, l in zip(cols[k2], ratio)]
+            g0, h0 = d * p - e * q, a * q - e * p
+            ai, ei, di = a * inv, e * inv, d * inv
+            ratio = [(g0 * inv, h0 * inv)]
+            ratio += [(di * v - ei * w, ai * w - ei * v) for v, w in zip(x[1:], y[1:])]
+            for k2 in range(k + 2, 8):
+                s, t = rows_of(p, k2), rows_of(q, k2)
+                new = [v - (g * s + h * t) for v, (g, h) in zip(cols[k2], ratio)]
+                if k2 < k + 4:
+                    new[0] = cols[k2][0] - (g0 * s + h0 * t) * inv
+                cols[k2] = new
+            for k2, v in enumerate(after):
+                g, h = ratio[1]
+                after[k2] = v - (g * rows_of(x[1], k2) + h * rows_of(y[1], k2))
+            u, w = rows_of(m[b], k), rows_of(m[b], k + 1)
+            ra = lax.rsqrt(a)
+            fresh = jnp.where(sub == k, u * ra, (w - (e * (ra * ra)) * u) * (a * ra * r))
+            done = fresh if done is None else jnp.where(sub < k, done, fresh)
             for i in range(b, nb):
-                m[i] = m[i] - ratio[i - b] * u
+                g, h = ratio[i - b]
+                m[i] = m[i] - (g * u + h * w)
         result.append(done[:, r1:])
+        diag = after
     return jnp.concatenate(result, axis=0)
 
 
-def iteration(g1, g2, g3, held, _, carry):
+def times_gram(a1, a2, a3, g1, g2, g3):
+    r1 = a1.shape[0]
+    t1 = dot(jnp.concatenate([a1, a2, a3], axis=0), g1[...])
+    t2 = dot(jnp.concatenate([a1, a2], axis=0), g2[...])
+    t3 = dot(a1, g3[...])
+    return t1[:r1] + ((t1[r1:2 * r1] + t2[:r1]) + (t1[2 * r1:] + t2[r1:] + t3))
+
+
+def iteration(g1, g2, g3, held, step, carry):
     r1 = held.shape[0]
-    f1, f2, f3 = split(held[...])
-    t1 = dot(jnp.concatenate([f1, f2, f3], axis=0), g1[...])
-    t2 = dot(jnp.concatenate([f1, f2], axis=0), g2[...])
-    t3 = dot(f1, g3[...])
-    a = t1[:r1] + ((t1[r1:2 * r1] + t2[:r1]) + (t1[2 * r1:] + t2[r1:] + t3))
-    a1, a2, a3 = split(a)
-    stack = jnp.concatenate([a1, a2, a3], axis=0)
+    a1, a2, a3 = split(held[...])
     c = dot(a1, a1, NT) + (
         dot(a1, a2, NT) + dot(a2, a1, NT) + (dot(a2, a2, NT) + dot(a1, a3, NT) + dot(a3, a1, NT))
     )
+    last = step == ITERS - 1
+    b = split(times_gram(a1, a2, a3, g1, g2, g3))
+    stack = jnp.concatenate([jnp.where(last, x, y) for x, y in zip((a1, a2, a3), b)], axis=0)
     w1, w2, w3 = split(inverse_lower(c))
     none = jnp.zeros_like(w1)
     t = dot(
@@ -209,7 +246,7 @@
 
 def iterate_kernel(g_ref, f_ref, out_ref, g1, g2, g3, held):
     g1[...], g2[...], g3[...] = split(g_ref[...])
-    held[...] = f_ref[...].T
+    held[...] = times_gram(*split(f_ref[...].T), g1, g2, g3)
     lax.fori_loop(0, ITERS, functools.partial(iteration, g1, g2, g3, held), 0)
     out_ref[...] = held[...].T
 
@@ -226,7 +263,7 @@
 
 
 def whole_kernel(ny, nz, chunk, jb, ahead, scale, x_ref, f_ref, factor_ref, out_ref,
-                 xs, acc, packed, got1, held, got2, mid, got3, full, g1, g2, g3, basis, weights,
+                 io, xs, acc, packed, got1, held, got2, mid, got3, full, g1, g2, g3, basis, weights,
                  raw, mine, z, gram, got4, part, got5, last,
                  xsem, s1, r1, s2, r2, s3, r3, s4, r4, s5, r5, s6, r6, sr, rr,
                  sa, ra, sb, rb, sc, rc, sd, rd):
@@ -254,6 +291,8 @@
     loads = [load(o) for o in range(ny)]
     for copy in loads:
         copy.start()
+    start = pltpu.make_async_copy(f_ref, basis, io.at[0])
+    start.start()
 
     size = 2 * LANES
     for o in range(ny):
@@ -339,10 +378,12 @@
         for a, b, value in ((i, j, block), (j, i, block.T))[:1 if i == j else 2]:
             where = (slice(a * LANES, (a + 1) * LANES), slice(b * LANES, (b + 1) * LANES))
             g1[where], g2[where], g3[where] = split(value)
-    basis[...] = f_ref[...]
+    start.wait()
+    basis[...] = times_gram(*split(basis[...]), g1, g2, g3)
     lax.fori_loop(0, ITERS, functools.partial(iteration, g1, g2, g3, basis), 0)
     factor = basis[...]
-    factor_ref[...] = factor
+    leave = pltpu.make_async_copy(basis, factor_ref, io.at[1])
+    leave.start()
     narrow = factor.T.astype(jnp.bfloat16)
     empty = jnp.zeros_like(narrow)
     weights[0] = jnp.concatenate([narrow, empty], axis=1)
@@ -394,10 +435,26 @@
         final[o] = send(last.at[gz], last.at[gz], sd.at[o], rd.at[o], (gy, planes[o]))
     for o in range(1, nz):
         final[o].wait_recv()
+    done = pltpu.make_async_copy(last, out_ref, io.at[2])
+    done.start()
     for group in (first, second, third, fourth, fifth, sixth, sent, across, planar, rowwise, final):
         for copy in group.values():
             copy.wait_send()
-    out_ref[...] = last[...]
+    leave.wait()
+    done.wait()
+
+
+def deliver_kernel(a_ref, b_ref, c_ref, d_ref):
+    c_ref[...] = a_ref[...]
+    d_ref[...] = b_ref[...]
+
+
+def deliver(a, b):
+    shape = jax.ShapeDtypeStruct
+    return pl.pallas_call(
+        deliver_kernel, out_shape=(shape(a.shape, a.dtype), shape(b.shape, b.dtype)),
+        in_specs=[VMEM, VMEM], out_specs=(VMEM, VMEM), name="deliver",
+    )(a, b)
 
 
 def whole(state_field, start_factor, divisor):
@@ -420,8 +477,9 @@
     factor, out = pl.pallas_call(
         functools.partial(whole_kernel, ny, nz, chunk, jb, ahead, 1.0 / divisor),
         out_shape=(jax.ShapeDtypeStruct((r1, n1), f32), jax.ShapeDtypeStruct((nz, q, j2), f32)),
-        in_specs=[pl.BlockSpec(memory_space=pl.ANY), VMEM], out_specs=(VMEM, VMEM),
+        in_specs=[ANY, ANY], out_specs=(ANY, ANY),
         scratch_shapes=[
+            dma((3,)),
             vmem((ny, 2, rows, n1), bf16),
             vmem((n1, n1), f32),
             vmem((chunk * ny * nz, LANES), f32),
@@ -450,6 +508,7 @@
         ),
         name="whole",
     )(halves, start_factor.T)
+    factor, out = deliver(factor, out)
     return factor.T, out.reshape(jb, j2)
 
 

time: 77.6 us -> 69.1 us (0.89)
  Pallas kernels: 73.8 us -> 68.3 us
  local copies, waits for them, and re-layouts: 2.94 us -> 0 us
    pallas_call x1, Pallas kernels: 73.8 us -> 66.7 us  [whole(): pl.pallas_call(functools.partial(whole_kernel, ny, nz, chunk, jb, ahead,...]
    unnamed x2 -> x0, local copies, waits for them, and re-layouts: 2.94 us -> none
    pallas_call x0 -> x1, Pallas kernels: none -> 1.57 us  [deliver(): pl.pallas_call(deliver_kernel, out_shape=(shape(a.shape, a.dtype), shape(...]
where the time goes in v1:
time: 69.1 us; the launch traced here: 68.9 us
  Pallas kernels  68.3 us (99%)
    pallas_call x1, Pallas kernels, whole(): pl.pallas_call(functools.partial(whole_kernel, ny, nz, chunk, jb, ahead,...  66.7 us
    pallas_call x1, Pallas kernels, deliver(): pl.pallas_call(deliver_kernel, out_shape=(shape(a.shape, a.dtype), shape(...  1.57 us

profile of v1, /device:TPU:0, one launch (start us, length us, event | category | flops | bytes accessed | tf_op | source)
XLA Modules:
  0.0 68.9 jit_solution(11962215780523022052)
XLA Ops:
  0.6 66.7 %whole.1 = (f32[64,512]{1,0:T(8,128)}, f32[4,8,256]{2,1,0:T(8,128)}) custom-call(bf16[2,2816,512]{2,1,0:T(8,128)(2,1)} %bitcast.4, f32[64,512]{1,0:T(8,128)} %bitcast.5), custom_call_target="tpu_custom_call" | custom-call | tf_op jit(solution)/shard_map/whole/pallas_call | solution.py:477
  67.3 1.6 %deliver.1 = (f32[64,512]{1,0:T(8,128)}, f32[4,8,256]{2,1,0:T(8,128)}) custom-call(f32[64,512]{1,0:T(8,128)} %get-tuple-element.6.a_ref, f32[4,8,256]{2,1,0:T(8,128)} %get-tuple-element.7.b_ref), custom_call_target="tpu_custom_call" | custom-call | tf_op jit(solution)/shard_map/deliver/pallas_call | solution.py:454

commit v2 on v1

--- a/solution.py
+++ b/solution.py
@@ -30,6 +30,10 @@
     )
     copy.start()
     return copy
+
+
+def settle(view, sem):
+    pltpu.make_async_copy(view, view, sem).wait()
 
 
 def sum_kernel(ny, nz, chunk, g_ref, out_ref, packed, got1, held, got2, mid, got3, full,
@@ -262,11 +266,21 @@
     )(mode_gram, start_factor)
 
 
+def tiles_of(n):
+    return [(i, j) for i in range(n) for j in range(i + 1, n)] + [(i, i) for i in range(n)]
+
+
+def blocks_of(n):
+    blocks = []
+    for i, j in tiles_of(n // 2):
+        blocks += [(2 * i + a, 2 * j + b) for a in range(2) for b in range(2) if i < j or a <= b]
+    return blocks
+
+
 def whole_kernel(ny, nz, chunk, jb, ahead, scale, x_ref, f_ref, factor_ref, out_ref,
-                 io, xs, acc, packed, got1, held, got2, mid, got3, full, g1, g2, g3, basis, weights,
+                 io, xs, packed, got1, held, got2, mid, got3, full, g1, g2, g3, basis, weights,
                  raw, mine, z, gram, got4, part, got5, last,
-                 xsem, s1, r1, s2, r2, s3, r3, s4, r4, s5, r5, s6, r6, sr, rr,
-                 sa, ra, sb, rb, sc, rc, sd, rd):
+                 xsem, left, r1, r2, r3, r4, r5, r6, rr, ra, rb, rc, rd):
     gy, gz = lax.axis_index("gy"), lax.axis_index("gz")
     depth = ny // 2
     zi, core = gy // 2, gy % 2
@@ -277,7 +291,6 @@
     rows = mine.shape[1]
     early = ahead * jb
     n1 = x_ref.shape[2]
-    copies = []
 
     barrier = pltpu.get_barrier_semaphore()
     greeted = [(p, gz) for p in peers[1:]] + [(gy, g) for g in planes[1:]]
@@ -286,7 +299,7 @@
 
     def load(o):
         src = x_ref.at[:, pl.ds(pl.multiple_of(peers[o] * rows, 8), rows)]
-        return pltpu.make_async_copy(src, xs.at[o], xsem.at[o])
+        return pltpu.make_async_copy(src, xs.at[o], xsem.at[2 * o // ny])
 
     loads = [load(o) for o in range(ny)]
     for copy in loads:
@@ -295,26 +308,62 @@
     start.start()
 
     size = 2 * LANES
-    for o in range(ny):
-        loads[o].wait()
-        for i in range(0, n1, size):
-            left = xs[o, :, :, i:i + size].reshape(2 * rows, size)
-            right = xs[o, :, :, i:].reshape(2 * rows, n1 - i)
-            value = dot(left, right, (((0,), (0,)), ((), ())))
-            if o:
-                acc[i:i + size, i:] += value
-            else:
-                acc[i:i + size, i:] = value
-
     n = n1 // LANES
-    blocks = [(i, j) for i in range(n) for j in range(i, n)]
-    for k, (i, j) in enumerate(blocks):
-        packed[k * LANES:(k + 1) * LANES, :] = acc[i * LANES:(i + 1) * LANES, j * LANES:(j + 1) * LANES]
-    used = len(blocks) * LANES
-    if used < packed.shape[0]:
-        packed[used:, :] = jnp.zeros((packed.shape[0] - used, LANES), jnp.float32)
-
+    blocks = blocks_of(n)
+    groups = len(blocks) // 2
+    order = {block: k for k, block in enumerate(blocks)}
+    wide_piece = LANES // nz
+    small = wide_piece // depth
+
+    def add_tile(i, j, low, high, start):
+        deep = (high - low) * 2 * rows
+        left = xs[low:high, :, :, i * size:(i + 1) * size].reshape(deep, size)
+        right = xs[low:high, :, :, j * size:(j + 1) * size].reshape(deep, size)
+        value = dot(left, right, (((0,), (0,)), ((), ())))
+        for a in range(2):
+            for b in range(2):
+                k = order.get((2 * i + a, 2 * j + b))
+                if k is not None:
+                    block = value[a * LANES:(a + 1) * LANES, b * LANES:(b + 1) * LANES]
+                    if start:
+                        packed[k] = block
+                    else:
+                        packed[k] += block
+
+    def pair_up(k):
+        send(packed.at[2 * k + 1 - core], got1.at[k], left.at[0], r1.at[k], partner)
+
+    def spread_plane(k):
+        settle(got1.at[k], r1.at[k])
+        held[k] = packed[2 * k + core] + got1[k]
+        for o in range(1, nz):
+            part_o = pl.ds(pl.multiple_of(planes[o] * wide_piece, 8), wide_piece)
+            send(held.at[k, part_o], got2.at[k, o - 1], left.at[1], r2.at[k], (gy, planes[o]))
+
+    tiles = tiles_of(n // 2)
+    half_way = ny // 2
+    for low in (0, half_way):
+        settle(xs.at[pl.ds(low, half_way)], xsem.at[low // half_way])
+        add_tile(*tiles[0], low, low + half_way, low == 0)
     pl.semaphore_wait(barrier, len(greeted))
+    for k in range(2):
+        pair_up(k)
+    for i, j in tiles[1:]:
+        for low in (0, half_way):
+            add_tile(i, j, low, low + half_way, low == 0)
+    for k in range(2, groups):
+        pair_up(k)
+    for k in range(groups):
+        spread_plane(k)
+    for k in range(groups):
+        total = held[k, pl.ds(pl.multiple_of(gz * wide_piece, 8), wide_piece), :]
+        settle(got2.at[k], r2.at[k])
+        for o in range(1, nz):
+            total = total + got2[k, o - 1]
+        mid[k] = total
+        for p in range(1, depth):
+            part_p = pl.ds(pl.multiple_of(stacks[p] * small, 8), small)
+            send(mid.at[k, part_p], got3.at[k, p - 1], left.at[2], r3.at[0], (2 * stacks[p] + core, gz))
 
     unit = nz * chunk
 
@@ -324,57 +373,37 @@
     def spot(half, q, g):
         return pl.ds(pl.multiple_of((half * depth + q) * unit + g * chunk, 8), chunk)
 
-    order = list(range(depth - 1, 0, -1)) + [0]
-    first, second, third = {}, {}, {}
-    for p in order:
-        first[p] = send(packed.at[span(1 - core, stacks[p])], got1.at[p], s1.at[p], r1.at[p], partner)
-    for p in order:
-        first[p].wait_recv()
-        held[p] = packed[span(core, stacks[p]), :] + got1[p]
-        for o in range(1, nz):
-            rows_o = pl.ds(pl.multiple_of(planes[o] * chunk, 8), chunk)
-            second[p, o] = send(held.at[p, rows_o], got2.at[p, o], s2.at[p, o], r2.at[p, o], (gy, planes[o]))
-    piece = None
-    for p in order:
-        total = held[p, pl.ds(pl.multiple_of(gz * chunk, 8), chunk), :]
-        for o in range(1, nz):
-            second[p, o].wait_recv()
-            total = total + got2[p, o]
-        if p:
-            mid[p] = total
-            third[p] = send(mid.at[p], got3.at[p], s3.at[p], r3.at[p], (2 * stacks[p] + core, gz))
-        else:
-            piece = total
+    base_row = (core * depth + zi) * unit + gz * chunk
+    settle(got3, r3.at[0])
+    for k in range(groups):
+        piece = mid[k, pl.ds(pl.multiple_of(zi * small, 8), small), :]
+        for p in range(1, depth):
+            piece = piece + got3[k, p - 1]
+        full[pl.ds(pl.multiple_of(base_row + k * small, 8), small), :] = piece
+    own = spot(core, zi, gz)
     for p in range(1, depth):
-        third[p].wait_recv()
-        piece = piece + got3[p]
-    own = spot(core, zi, gz)
-    full[own, :] = piece
-    fourth, fifth, sixth = {}, {}, {}
-    for p in range(1, depth):
-        fourth[p] = send(full.at[own], full.at[own], s4.at[p], r4.at[p], (2 * stacks[p] + core, gz))
+        send(full.at[own], full.at[own], left.at[3], r4.at[p - 1], (2 * stacks[p] + core, gz))
     came = [lax.rem(zi + depth - p, depth) for p in range(depth)]
     for p in range(depth):
         if p:
-            fourth[p].wait_recv()
+            settle(full.at[pl.ds(0, chunk)], r4.at[p - 1])
         here = spot(core, came[p], gz)
         for o in range(1, nz):
-            fifth[p, o] = send(full.at[here], full.at[here], s5.at[p, o], r5.at[p, o], (gy, planes[o]))
+            send(full.at[here], full.at[here], left.at[4], r5.at[p], (gy, planes[o]))
     for p in range(depth):
-        for o in range(1, nz):
-            fifth[p, o].wait_recv()
+        settle(full.at[pl.ds(0, (nz - 1) * chunk)], r5.at[p])
         here = span(core, came[p])
-        sixth[p] = send(full.at[here], full.at[here], s6.at[p], r6.at[p], partner)
-    for p in range(depth):
-        sixth[p].wait_recv()
-
-    sent = {}
+        send(full.at[here], full.at[here], left.at[5], r6.at[0], partner)
+    settle(full.at[pl.ds(0, depth * unit)], r6.at[0])
+
+    far = list(range(ny // 2, ny)) + list(range(ny // 2 - 1, 0, -1))
     if ahead:
-        for o in range(1, ny):
-            sent[o] = send(xs.at[o, :, pl.ds(0, early)], raw.at[gy], sr.at[o], rr.at[o], (peers[o], gz))
+        for o in far:
+            send(xs.at[o, :, pl.ds(0, early)], raw.at[gy], left.at[6], rr.at[0], (peers[o], gz))
 
     for k, (i, j) in enumerate(blocks):
-        block = full[k * LANES:(k + 1) * LANES, :]
+        rows_k = [((k % 2 * depth + q) * nz + g) * chunk + k // 2 * small for g in range(nz) for q in range(depth)]
+        block = jnp.concatenate([full[row:row + small, :] for row in rows_k], axis=0)
         for a, b, value in ((i, j, block), (j, i, block.T))[:1 if i == j else 2]:
             where = (slice(a * LANES, (a + 1) * LANES), slice(b * LANES, (b + 1) * LANES))
             g1[where], g2[where], g3[where] = split(value)
@@ -392,54 +421,50 @@
     def project(pair):
         return (dot(pair[0], weights[0]) + dot(pair[1], weights[1])).astype(jnp.bfloat16)
 
-    across = {}
-    far = list(range(ny // 2, ny)) + list(range(ny // 2 - 1, 0, -1))
+    late = pl.ds(early, rows - early)
     for o in far:
         mine[o, early:] = project(xs[o, :, early:])
-        across[o] = send(
-            mine.at[o, pl.ds(early, rows - early)], z.at[gy, pl.ds(early, rows - early)],
-            sa.at[o], ra.at[o], (peers[o], gz),
-        )
+        send(mine.at[o, late], z.at[gy, late], left.at[7], ra.at[0], (peers[o], gz))
     z[gy] = project(xs[0])
     if ahead:
+        settle(raw.at[pl.ds(0, ny - 1)], rr.at[0])
         for o in range(1, ny):
-            sent[o].wait_recv()
             source = lax.rem(gy + ny - o, ny)
             z[source, :early] = project(raw[source])
-    for o in range(1, ny):
-        across[o].wait_recv()
+    settle(z.at[pl.ds(0, ny - 1), late], ra.at[0])
     wide = jnp.concatenate(
         [z[:, t * jb:(t + 1) * jb, :].reshape(ny * jb, LANES) for t in range(rows // jb)], axis=1
     )
     gram[...] = dot(wide, wide, NT).reshape(gram.shape)
-    planar, rowwise, final = {}, {}, {}
     far = far + [0]
     for o in far:
         for g in range(1, nz):
-            planar[o, g] = send(
-                gram.at[peers[o], planes[g]], got4.at[o, g], sb.at[o, g], rb.at[o, g], (gy, planes[g])
-            )
+            send(gram.at[peers[o], planes[g]], got4.at[o, g - 1], left.at[8], rb.at[o], (gy, planes[g]))
     for o in far:
+        settle(got4.at[o], rb.at[o])
         total = gram[peers[o], gz]
         for g in range(1, nz):
-            planar[o, g].wait_recv()
-            total = total + got4[o, g]
+            total = total + got4[o, g - 1]
         if o:
-            part[o] = total
-            rowwise[o] = send(part.at[o], got5.at[o], sc.at[o], rc.at[o], (peers[o], gz))
+            part[o - 1] = total
+            send(part.at[o - 1], got5.at[o - 1], left.at[9], rc.at[0], (peers[o], gz))
+    settle(got5, rc.at[0])
     for o in range(1, ny):
-        rowwise[o].wait_recv()
-        total = total + got5[o]
+        total = total + got5[o - 1]
     last[gz] = total * scale
     for o in range(1, nz):
-        final[o] = send(last.at[gz], last.at[gz], sd.at[o], rd.at[o], (gy, planes[o]))
-    for o in range(1, nz):
-        final[o].wait_recv()
+        send(last.at[gz], last.at[gz], left.at[10], rd.at[0], (gy, planes[o]))
+    settle(last.at[pl.ds(0, nz - 1)], rd.at[0])
     done = pltpu.make_async_copy(last, out_ref, io.at[2])
     done.start()
-    for group in (first, second, third, fourth, fifth, sixth, sent, across, planar, rowwise, final):
-        for copy in group.values():
-            copy.wait_send()
+    gone = [
+        got1, got2, got3, full.at[pl.ds(0, (depth - 1) * chunk)], full.at[pl.ds(0, depth * (nz - 1) * chunk)],
+        full.at[pl.ds(0, depth * unit)], raw.at[pl.ds(0, ny - 1)], z.at[pl.ds(0, ny - 1), late], got4, got5,
+        last.at[pl.ds(0, nz - 1)],
+    ]
+    for k, view in enumerate(gone):
+        if ahead or k != 6:
+            settle(view, left.at[k])
     leave.wait()
     done.wait()
 
@@ -466,10 +491,10 @@
     ahead = AHEAD
     halves = state_field.reshape(2, half * jb, n1)
     n = n1 // LANES
-    used = n * (n + 1) // 2 * LANES
-    chunk = -(-used // (8 * ny * nz)) * 8
+    groups = n * (n + 1) // 4
     depth = ny // 2
-    unit = nz * chunk
+    small = LANES // (nz * depth)
+    chunk = groups * small
     q, j2 = jb // nz, ny * jb
     f32, bf16 = jnp.float32, jnp.bfloat16
     dma = pltpu.SemaphoreType.DMA
@@ -481,13 +506,12 @@
         scratch_shapes=[
             dma((3,)),
             vmem((ny, 2, rows, n1), bf16),
-            vmem((n1, n1), f32),
-            vmem((chunk * ny * nz, LANES), f32),
-            vmem((depth, unit, LANES), f32),
-            vmem((depth, unit, LANES), f32),
-            vmem((depth, nz, chunk, LANES), f32),
-            vmem((depth, chunk, LANES), f32),
-            vmem((depth, chunk, LANES), f32),
+            vmem((2 * groups, LANES, LANES), f32),
+            vmem((groups, LANES, LANES), f32),
+            vmem((groups, LANES, LANES), f32),
+            vmem((groups, nz - 1, LANES // nz, LANES), f32),
+            vmem((groups, LANES // nz, LANES), f32),
+            vmem((groups, depth - 1, small, LANES), f32),
             vmem((chunk * ny * nz, LANES), f32),
             vmem((n1, n1), bf16), vmem((n1, n1), bf16), vmem((n1, n1), bf16),
             vmem((r1, n1), f32),
@@ -496,13 +520,13 @@
             vmem((ny, rows, LANES), bf16),
             vmem((ny, rows, LANES), bf16),
             vmem((ny, nz, q, j2), f32),
-            vmem((ny, nz, q, j2), f32),
-            vmem((ny, q, j2), f32),
-            vmem((ny, q, j2), f32),
+            vmem((ny, nz - 1, q, j2), f32),
+            vmem((ny - 1, q, j2), f32),
+            vmem((ny - 1, q, j2), f32),
             vmem((nz, q, j2), f32),
-            dma((ny,)),
-        ] + [dma((depth,))] * 2 + [dma((depth, nz))] * 2 + [dma((depth,))] * 4 + [dma((depth, nz))] * 2
-        + [dma((depth,))] * 2 + [dma((ny,))] * 4 + [dma((ny, nz))] * 2 + [dma((ny,))] * 2 + [dma((nz,))] * 2,
+            dma((2,)), dma((11,)), dma((groups,)), dma((groups,)), dma((1,)), dma((depth - 1,)), dma((depth,)),
+            dma((1,)), dma((1,)), dma((1,)), dma((ny,)), dma((1,)), dma((1,)),
+        ],
         compiler_params=pltpu.CompilerParams(
             collective_id=1, has_side_effects=True, vmem_limit_bytes=56 * 2**20
         ),
@@ -527,7 +551,8 @@
     nv, nk, jb, n1 = state_field.shape
     r1 = start_factor.shape[1]
     divisor = nv * nk * nz * r1
-    if (nv * nk) % (2 * ny) == 0 and jb % (8 * nz) == 0 and 2 * r1 == LANES and n1 % (2 * LANES) == 0:
+    halves = (nv * nk) % (2 * ny) == 0 and jb % (8 * nz) == 0 and 2 * r1 == LANES
+    if halves and n1 % (4 * LANES) == 0 and ny % 4 == 0 and LANES % (4 * ny * nz) == 0:
         return whole(state_field, start_factor, divisor)
     flattened = state_field.reshape(-1, n1)
     partial_value = dot(flattened, flattened, (((0,), (0,)), ((), ())))

time: 69.1 us -> 66.4 us (0.961)
  Pallas kernels: 68.3 us -> 65.6 us
    pallas_call x1, Pallas kernels: 66.7 us -> 64.1 us  [whole(): pl.pallas_call(functools.partial(whole_kernel, ny, nz, chunk, jb, ahead,...]
where the time goes in v2:
time: 66.4 us; the launch traced here: 66.3 us
  Pallas kernels  65.6 us (99%)
    pallas_call x1, Pallas kernels, whole(): pl.pallas_call(functools.partial(whole_kernel, ny, nz, chunk, jb, ahead,...  64.1 us
    pallas_call x1, Pallas kernels, deliver(): pl.pallas_call(deliver_kernel, out_shape=(shape(a.shape, a.dtype), shape(...  1.57 us

profile of v2, /device:TPU:0, one launch (start us, length us, event | category | flops | bytes accessed | tf_op | source)
XLA Modules:
  0.0 66.3 jit_solution(15343800032109709717)
XLA Ops:
  0.6 64.1 %whole.1 = (f32[64,512]{1,0:T(8,128)}, f32[4,8,256]{2,1,0:T(8,128)}) custom-call(bf16[2,2816,512]{2,1,0:T(8,128)(2,1)} %bitcast.4, f32[64,512]{1,0:T(8,128)} %bitcast.5), custom_call_target="tpu_custom_call" | custom-call | tf_op jit(solution)/shard_map/whole/pallas_call | solution.py:502
  64.7 1.6 %deliver.1 = (f32[64,512]{1,0:T(8,128)}, f32[4,8,256]{2,1,0:T(8,128)}) custom-call(f32[64,512]{1,0:T(8,128)} %get-tuple-element.6.a_ref, f32[4,8,256]{2,1,0:T(8,128)} %get-tuple-element.7.b_ref), custom_call_target="tpu_custom_call" | custom-call | tf_op jit(solution)/shard_map/deliver/pallas_call | solution.py:479

commit v3 on v2

--- a/solution.py
+++ b/solution.py
@@ -8,7 +8,8 @@
 from jax.sharding import PartitionSpec as P
 
 ITERS = 6
-AHEAD = 1
+EARLY = (4, 5)
+TWICE = (4, 5)
 MESH = pl.DeviceIdType.MESH
 LANES = 128
 VMEM = pl.BlockSpec(memory_space=pltpu.VMEM)
@@ -225,9 +226,10 @@
 def iteration(g1, g2, g3, held, step, carry):
     r1 = held.shape[0]
     a1, a2, a3 = split(held[...])
-    c = dot(a1, a1, NT) + (
-        dot(a1, a2, NT) + dot(a2, a1, NT) + (dot(a2, a2, NT) + dot(a1, a3, NT) + dot(a3, a1, NT))
-    )
+    p1 = dot(jnp.concatenate([a1, a2, a3], axis=0), a1, NT)
+    p2 = dot(jnp.concatenate([a1, a2], axis=0), a2, NT)
+    p3 = dot(a1, a3, NT)
+    c = p1[:r1] + (p2[:r1] + p1[r1:2 * r1] + (p2[r1:] + p3 + p1[2 * r1:]))
     last = step == ITERS - 1
     b = split(times_gram(a1, a2, a3, g1, g2, g3))
     stack = jnp.concatenate([jnp.where(last, x, y) for x, y in zip((a1, a2, a3), b)], axis=0)
@@ -266,6 +268,11 @@
     )(mode_gram, start_factor)
 
 
+def batches_of(groups):
+    early = groups - 2
+    return [list(range(early)), list(range(early, groups))] if early > 0 else [list(range(groups))]
+
+
 def tiles_of(n):
     return [(i, j) for i in range(n) for j in range(i + 1, n)] + [(i, i) for i in range(n)]
 
@@ -277,9 +284,9 @@
     return blocks
 
 
-def whole_kernel(ny, nz, chunk, jb, ahead, scale, x_ref, f_ref, factor_ref, out_ref,
+def whole_kernel(ny, nz, jb, scale, x_ref, f_ref, factor_ref, out_ref,
                  io, xs, packed, got1, held, got2, mid, got3, full, g1, g2, g3, basis, weights,
-                 raw, mine, z, gram, got4, part, got5, last,
+                 raw, more, mine, z, gram, got4, part, got5, last,
                  xsem, left, r1, r2, r3, r4, r5, r6, rr, ra, rb, rc, rd):
     gy, gz = lax.axis_index("gy"), lax.axis_index("gz")
     depth = ny // 2
@@ -289,7 +296,10 @@
     stacks = [lax.rem(zi + p, depth) for p in range(depth)]
     peers = [lax.rem(gy + o, ny) for o in range(ny)]
     rows = mine.shape[1]
-    early = ahead * jb
+    soon = [o for o in EARLY if 0 < o < ny]
+    twice = [o for o in TWICE if 0 < o < ny]
+    once = [o for o in range(1, ny) if o not in twice]
+    first_rows, next_rows = pl.ds(0, jb), pl.ds(jb, jb)
     n1 = x_ref.shape[2]
 
     barrier = pltpu.get_barrier_semaphore()
@@ -314,6 +324,8 @@
     order = {block: k for k, block in enumerate(blocks)}
     wide_piece = LANES // nz
     small = wide_piece // depth
+    batches = batches_of(groups)
+    batch_of = {k: b for b, batch in enumerate(batches) for k in batch}
 
     def add_tile(i, j, low, high, start):
         deep = (high - low) * 2 * rows
@@ -346,8 +358,13 @@
         settle(xs.at[pl.ds(low, half_way)], xsem.at[low // half_way])
         add_tile(*tiles[0], low, low + half_way, low == 0)
     pl.semaphore_wait(barrier, len(greeted))
+    def send_raw(o):
+        send(xs.at[o, :, first_rows], raw.at[gy], left.at[6], rr.at[0], (peers[o], gz))
+
     for k in range(2):
         pair_up(k)
+    for o in soon:
+        send_raw(o)
     for i, j in tiles[1:]:
         for low in (0, half_way):
             add_tile(i, j, low, low + half_way, low == 0)
@@ -363,46 +380,55 @@
         mid[k] = total
         for p in range(1, depth):
             part_p = pl.ds(pl.multiple_of(stacks[p] * small, 8), small)
-            send(mid.at[k, part_p], got3.at[k, p - 1], left.at[2], r3.at[0], (2 * stacks[p] + core, gz))
-
-    unit = nz * chunk
-
-    def span(half, q):
-        return pl.ds(pl.multiple_of((half * depth + q) * unit, 8), unit)
-
-    def spot(half, q, g):
-        return pl.ds(pl.multiple_of((half * depth + q) * unit + g * chunk, 8), chunk)
-
-    base_row = (core * depth + zi) * unit + gz * chunk
-    settle(got3, r3.at[0])
-    for k in range(groups):
-        piece = mid[k, pl.ds(pl.multiple_of(zi * small, 8), small), :]
+            send(mid.at[k, part_p], got3.at[k, p - 1], left.at[2], r3.at[batch_of[k]], (2 * stacks[p] + core, gz))
+
+    pieces = 2 * depth * nz
+
+    def span(b, half, q, g=0, count=nz):
+        chunk = len(batches[b]) * small
+        start = batches[b][0] * small * pieces
+        return pl.ds(pl.multiple_of(start + ((half * depth + q) * nz + g) * chunk, 8), count * chunk)
+
+    def some(b, count):
+        return full.at[pl.ds(0, count * len(batches[b]) * small)]
+
+    for b, batch in enumerate(batches):
+        settle(got3.at[pl.ds(batch[0], len(batch))], r3.at[b])
+        total = mid[batch[0]:batch[-1] + 1, pl.ds(pl.multiple_of(zi * small, 8), small), :]
         for p in range(1, depth):
-            piece = piece + got3[k, p - 1]
-        full[pl.ds(pl.multiple_of(base_row + k * small, 8), small), :] = piece
-    own = spot(core, zi, gz)
-    for p in range(1, depth):
-        send(full.at[own], full.at[own], left.at[3], r4.at[p - 1], (2 * stacks[p] + core, gz))
+            total = total + got3[batch[0]:batch[-1] + 1, p - 1]
+        own = span(b, core, zi, gz, 1)
+        full[own, :] = total.reshape(len(batch) * small, LANES)
+        for p in range(1, depth):
+            send(full.at[own], full.at[own], left.at[3], r4.at[b, p - 1], (2 * stacks[p] + core, gz))
     came = [lax.rem(zi + depth - p, depth) for p in range(depth)]
-    for p in range(depth):
-        if p:
-            settle(full.at[pl.ds(0, chunk)], r4.at[p - 1])
-        here = spot(core, came[p], gz)
-        for o in range(1, nz):
-            send(full.at[here], full.at[here], left.at[4], r5.at[p], (gy, planes[o]))
-    for p in range(depth):
-        settle(full.at[pl.ds(0, (nz - 1) * chunk)], r5.at[p])
-        here = span(core, came[p])
-        send(full.at[here], full.at[here], left.at[5], r6.at[0], partner)
-    settle(full.at[pl.ds(0, depth * unit)], r6.at[0])
+    for b in range(len(batches)):
+        for p in range(depth):
+            if p:
+                settle(some(b, 1), r4.at[b, p - 1])
+            here = span(b, core, came[p], gz, 1)
+            for o in range(1, nz):
+                send(full.at[here], full.at[here], left.at[4], r5.at[b, p], (gy, planes[o]))
+    for b in range(len(batches)):
+        for p in range(depth):
+            settle(some(b, nz - 1), r5.at[b, p])
+            here = span(b, core, came[p])
+            send(full.at[here], full.at[here], left.at[5], r6.at[0], partner)
+    rows_full = pieces * groups * small
+    settle(full.at[pl.ds(0, rows_full // 2)], r6.at[0])
 
     far = list(range(ny // 2, ny)) + list(range(ny // 2 - 1, 0, -1))
-    if ahead:
-        for o in far:
-            send(xs.at[o, :, pl.ds(0, early)], raw.at[gy], left.at[6], rr.at[0], (peers[o], gz))
+    for o in far:
+        if o not in soon:
+            send_raw(o)
+    for o in twice:
+        send(xs.at[o, :, next_rows], more.at[gy], left.at[11], rr.at[1], (peers[o], gz))
 
     for k, (i, j) in enumerate(blocks):
-        rows_k = [((k % 2 * depth + q) * nz + g) * chunk + k // 2 * small for g in range(nz) for q in range(depth)]
+        batch = batches[batch_of[k // 2]]
+        chunk = len(batch) * small
+        at = batch[0] * small * pieces + (k // 2 - batch[0]) * small
+        rows_k = [at + ((k % 2 * depth + q) * nz + g) * chunk for g in range(nz) for q in range(depth)]
         block = jnp.concatenate([full[row:row + small, :] for row in rows_k], axis=0)
         for a, b, value in ((i, j, block), (j, i, block.T))[:1 if i == j else 2]:
             where = (slice(a * LANES, (a + 1) * LANES), slice(b * LANES, (b + 1) * LANES))
@@ -421,17 +447,25 @@
     def project(pair):
         return (dot(pair[0], weights[0]) + dot(pair[1], weights[1])).astype(jnp.bfloat16)
 
-    late = pl.ds(early, rows - early)
+    ranges = {o: pl.ds(2 * jb, rows - 2 * jb) if o in twice else pl.ds(jb, rows - jb) for o in far}
     for o in far:
-        mine[o, early:] = project(xs[o, :, early:])
-        send(mine.at[o, late], z.at[gy, late], left.at[7], ra.at[0], (peers[o], gz))
+        late, kind = ranges[o], int(o in twice)
+        mine[o, late] = project(xs[o, :, late])
+        send(mine.at[o, late], z.at[gy, late], left.at[12 if kind else 7], ra.at[kind], (peers[o], gz))
     z[gy] = project(xs[0])
-    if ahead:
-        settle(raw.at[pl.ds(0, ny - 1)], rr.at[0])
-        for o in range(1, ny):
-            source = lax.rem(gy + ny - o, ny)
-            z[source, :early] = project(raw[source])
-    settle(z.at[pl.ds(0, ny - 1), late], ra.at[0])
+    settle(raw.at[pl.ds(0, ny - 1)], rr.at[0])
+    for o in range(1, ny):
+        z[peers[o], first_rows] = project(raw[peers[o]])
+    if twice:
+        settle(more.at[pl.ds(0, len(twice))], rr.at[1])
+    for o in twice:
+        source = lax.rem(gy + ny - o, ny)
+        z[source, next_rows] = project(more[source])
+    whole_once = z.at[pl.ds(0, len(once)), pl.ds(jb, rows - jb)]
+    settle(whole_once, ra.at[0])
+    whole_twice = z.at[pl.ds(0, max(len(twice), 1)), pl.ds(2 * jb, rows - 2 * jb)]
+    if twice:
+        settle(whole_twice, ra.at[1])
     wide = jnp.concatenate(
         [z[:, t * jb:(t + 1) * jb, :].reshape(ny * jb, LANES) for t in range(rows // jb)], axis=1
     )
@@ -458,13 +492,14 @@
     done = pltpu.make_async_copy(last, out_ref, io.at[2])
     done.start()
     gone = [
-        got1, got2, got3, full.at[pl.ds(0, (depth - 1) * chunk)], full.at[pl.ds(0, depth * (nz - 1) * chunk)],
-        full.at[pl.ds(0, depth * unit)], raw.at[pl.ds(0, ny - 1)], z.at[pl.ds(0, ny - 1), late], got4, got5,
+        got1, got2, got3, full.at[pl.ds(0, (depth - 1) * groups * small)],
+        full.at[pl.ds(0, depth * (nz - 1) * groups * small)], full.at[pl.ds(0, rows_full // 2)], raw.at[pl.ds(0, ny - 1)], whole_once, got4, got5,
         last.at[pl.ds(0, nz - 1)],
     ]
+    if twice:
+        gone += [more.at[pl.ds(0, len(twice))], whole_twice]
     for k, view in enumerate(gone):
-        if ahead or k != 6:
-            settle(view, left.at[k])
+        settle(view, left.at[k])
     leave.wait()
     done.wait()
 
@@ -488,19 +523,18 @@
     r1 = start_factor.shape[1]
     half = nv * nk // 2
     rows = half // ny * jb
-    ahead = AHEAD
     halves = state_field.reshape(2, half * jb, n1)
     n = n1 // LANES
     groups = n * (n + 1) // 4
     depth = ny // 2
     small = LANES // (nz * depth)
-    chunk = groups * small
+    count = len(batches_of(groups))
     q, j2 = jb // nz, ny * jb
     f32, bf16 = jnp.float32, jnp.bfloat16
     dma = pltpu.SemaphoreType.DMA
     vmem = pltpu.VMEM
     factor, out = pl.pallas_call(
-        functools.partial(whole_kernel, ny, nz, chunk, jb, ahead, 1.0 / divisor),
+        functools.partial(whole_kernel, ny, nz, jb, 1.0 / divisor),
         out_shape=(jax.ShapeDtypeStruct((r1, n1), f32), jax.ShapeDtypeStruct((nz, q, j2), f32)),
         in_specs=[ANY, ANY], out_specs=(ANY, ANY),
         scratch_shapes=[
@@ -512,11 +546,12 @@
             vmem((groups, nz - 1, LANES // nz, LANES), f32),
             vmem((groups, LANES // nz, LANES), f32),
             vmem((groups, depth - 1, small, LANES), f32),
-            vmem((chunk * ny * nz, LANES), f32),
+            vmem((groups * small * ny * nz, LANES), f32),
             vmem((n1, n1), bf16), vmem((n1, n1), bf16), vmem((n1, n1), bf16),
             vmem((r1, n1), f32),
             vmem((2, n1, LANES), bf16),
-            vmem((ny, 2, max(ahead, 1) * jb, n1), bf16),
+            vmem((ny, 2, jb, n1), bf16),
+            vmem((ny, 2, jb, n1), bf16),
             vmem((ny, rows, LANES), bf16),
             vmem((ny, rows, LANES), bf16),
             vmem((ny, nz, q, j2), f32),
@@ -524,8 +559,9 @@
             vmem((ny - 1, q, j2), f32),
             vmem((ny - 1, q, j2), f32),
             vmem((nz, q, j2), f32),
-            dma((2,)), dma((11,)), dma((groups,)), dma((groups,)), dma((1,)), dma((depth - 1,)), dma((depth,)),
-            dma((1,)), dma((1,)), dma((1,)), dma((ny,)), dma((1,)), dma((1,)),
+            dma((2,)), dma((13,)), dma((groups,)), dma((groups,)), dma((count,)), dma((count, depth - 1)),
+            dma((count, depth)),
+            dma((1,)), dma((2,)), dma((2,)), dma((ny,)), dma((1,)), dma((1,)),
         ],
         compiler_params=pltpu.CompilerParams(
             collective_id=1, has_side_effects=True, vmem_limit_bytes=56 * 2**20

time: 66.4 us -> 65.2 us (0.982)
  Pallas kernels: 65.6 us -> 64.4 us
    pallas_call x1, Pallas kernels: 64.1 us -> 62.9 us  [whole(): pl.pallas_call(functools.partial(whole_kernel, ny, nz, jb, 1.0 / divisor)...]
where the time goes in v3:
time: 65.2 us; the launch traced here: 65.1 us
  Pallas kernels  64.4 us (99%)
    pallas_call x1, Pallas kernels, whole(): pl.pallas_call(functools.partial(whole_kernel, ny, nz, jb, 1.0 / divisor)...  62.9 us
    pallas_call x1, Pallas kernels, deliver(): pl.pallas_call(deliver_kernel, out_shape=(shape(a.shape, a.dtype), shape(...  1.57 us

profile of v3, /device:TPU:0, one launch (start us, length us, event | category | flops | bytes accessed | tf_op | source)
XLA Modules:
  0.0 65.1 jit_solution(2441872004470897689)
XLA Ops:
  0.6 62.9 %whole.1 = (f32[64,512]{1,0:T(8,128)}, f32[4,8,256]{2,1,0:T(8,128)}) custom-call(bf16[2,2816,512]{2,1,0:T(8,128)(2,1)} %bitcast.4, f32[64,512]{1,0:T(8,128)} %bitcast.5), custom_call_target="tpu_custom_call" | custom-call | tf_op jit(solution)/shard_map/whole/pallas_call | solution.py:536
  63.5 1.6 %deliver.1 = (f32[64,512]{1,0:T(8,128)}, f32[4,8,256]{2,1,0:T(8,128)}) custom-call(f32[64,512]{1,0:T(8,128)} %get-tuple-element.6.a_ref, f32[4,8,256]{2,1,0:T(8,128)} %get-tuple-element.7.b_ref), custom_call_target="tpu_custom_call" | custom-call | tf_op jit(solution)/shard_map/deliver/pallas_call | solution.py:514

commit v4 on v3

--- a/solution.py
+++ b/solution.py
@@ -437,8 +437,7 @@
     basis[...] = times_gram(*split(basis[...]), g1, g2, g3)
     lax.fori_loop(0, ITERS, functools.partial(iteration, g1, g2, g3, basis), 0)
     factor = basis[...]
-    leave = pltpu.make_async_copy(basis, factor_ref, io.at[1])
-    leave.start()
+    factor_ref[...] = factor
     narrow = factor.T.astype(jnp.bfloat16)
     empty = jnp.zeros_like(narrow)
     weights[0] = jnp.concatenate([narrow, empty], axis=1)
@@ -489,8 +488,7 @@
     for o in range(1, nz):
         send(last.at[gz], last.at[gz], left.at[10], rd.at[0], (gy, planes[o]))
     settle(last.at[pl.ds(0, nz - 1)], rd.at[0])
-    done = pltpu.make_async_copy(last, out_ref, io.at[2])
-    done.start()
+    out_ref[...] = last[...]
     gone = [
         got1, got2, got3, full.at[pl.ds(0, (depth - 1) * groups * small)],
         full.at[pl.ds(0, depth * (nz - 1) * groups * small)], full.at[pl.ds(0, rows_full // 2)], raw.at[pl.ds(0, ny - 1)], whole_once, got4, got5,
@@ -500,20 +498,22 @@
         gone += [more.at[pl.ds(0, len(twice))], whole_twice]
     for k, view in enumerate(gone):
         settle(view, left.at[k])
-    leave.wait()
-    done.wait()
-
-
-def deliver_kernel(a_ref, b_ref, c_ref, d_ref):
-    c_ref[...] = a_ref[...]
-    d_ref[...] = b_ref[...]
+
+
+def deliver_kernel(a_ref, b_ref, c_ref, d_ref, sem):
+    left = [pltpu.make_async_copy(a_ref, c_ref, sem.at[0]), pltpu.make_async_copy(b_ref, d_ref, sem.at[1])]
+    for copy in left:
+        copy.start()
+    for copy in left:
+        copy.wait()
 
 
 def deliver(a, b):
     shape = jax.ShapeDtypeStruct
     return pl.pallas_call(
         deliver_kernel, out_shape=(shape(a.shape, a.dtype), shape(b.shape, b.dtype)),
-        in_specs=[VMEM, VMEM], out_specs=(VMEM, VMEM), name="deliver",
+        in_specs=[VMEM, VMEM], out_specs=(ANY, ANY), name="deliver",
+        scratch_shapes=[pltpu.SemaphoreType.DMA((2,))],
     )(a, b)
 
 
@@ -535,10 +535,10 @@
     vmem = pltpu.VMEM
     factor, out = pl.pallas_call(
         functools.partial(whole_kernel, ny, nz, jb, 1.0 / divisor),
-        out_shape=(jax.ShapeDtypeStruct((r1, n1), f32), jax.ShapeDtypeStruct((nz, q, j2), f32)),
-        in_specs=[ANY, ANY], out_specs=(ANY, ANY),
+        out_shape=(pltpu.VMEM((r1, n1), f32), pltpu.VMEM((nz, q, j2), f32)),
+        in_specs=[ANY, ANY], out_specs=(VMEM, VMEM),
         scratch_shapes=[
-            dma((3,)),
+            dma((1,)),
             vmem((ny, 2, rows, n1), bf16),
             vmem((2 * groups, LANES, LANES), f32),
             vmem((groups, LANES, LANES), f32),
@@ -568,6 +568,8 @@
         ),
         name="whole",
     )(halves, start_factor.T)
+    factor = pltpu.with_memory_space_constraint(factor, pltpu.VMEM)
+    out = pltpu.with_memory_space_constraint(out, pltpu.VMEM)
     factor, out = deliver(factor, out)
     return factor.T, out.reshape(jb, j2)
 

time: 65.2 us -> 63.7 us (0.977)
  Pallas kernels: 64.4 us -> 62.9 us
    pallas_call x1, Pallas kernels: 1.57 us -> 0.68 us  [deliver(): pl.pallas_call(deliver_kernel, out_shape=(shape(a.shape, a.dtype), shape(...]
where the time goes in v4:
time: 63.7 us; the launch traced here: 63.6 us
  Pallas kernels  62.9 us (99%)
  between operations  0.64 us (1%)
    pallas_call x1, Pallas kernels, whole(): pl.pallas_call(functools.partial(whole_kernel, ny, nz, jb, 1.0 / divisor)...  62.3 us

profile of v4, /device:TPU:0, one launch (start us, length us, event | category | flops | bytes accessed | tf_op | source)
XLA Modules:
  0.0 63.6 jit_solution(15630728531875552082)
XLA Ops:
  0.6 62.3 %whole.1 = (f32[64,512]{1,0:T(8,128)S(1)}, f32[4,8,256]{2,1,0:T(8,128)S(1)}) custom-call(bf16[2,2816,512]{2,1,0:T(8,128)(2,1)} %bitcast.4, f32[64,512]{1,0:T(8,128)} %bitcast.5), custom_call_target="tpu_custom_call" | custom-call | tf_op jit(solution)/shard_map/whole/pallas_call | solution.py:536
  62.9 0.7 %deliver.1 = (f32[64,512]{1,0:T(8,128)}, f32[4,8,256]{2,1,0:T(8,128)}) custom-call(f32[64,512]{1,0:T(8,128)S(1)} %get-tuple-element.6.a_ref, f32[4,8,256]{2,1,0:T(8,128)S(1)} %get-tuple-element.7.b_ref), custom_call_target="tpu_custom_call" | custom-call | tf_op jit(solution)/shard_map/deliver/pallas_call | solution.py:513
